TPU v7x, 512 devices: a whole 4x8x8 slice. The times are simulated.
512 devices in a mesh: ctx: 64 (over z_lo, y, core), head: 8 (over z_hi, x).
Axes of the slice: x: 4, y: 8, z: 8 (z_hi: 2, z_lo: 4; z = z_hi * 4 + z_lo), core: 2. Of those that a mesh axis runs over, the one named last changes fastest.
Arguments:
- frozen_queries: bfloat16 [8192, 12288], P('ctx', 'head'), may hold values from -20.4 to 20.4
- query_latent_rows: bfloat16 [8192, 1536], P('ctx'), may hold values from -6 to 6
- key_value_latent: bfloat16 [8192, 576], P('ctx'), may hold values from -20.4 to 20.4
- block_starts: int32 [64, 2], P('ctx'), may hold values from 0 to 960, as said below
- latent_up_weight: bfloat16 [512, 16384], P(None, 'head'), may hold values from -0.25 to 0.25
- query_adapter_first: bfloat16 [1536, 32], replicated, may hold values from -0.15625 to 0.15625
- query_adapter_second: bfloat16 [32, 12288], P(None, 'head'), may hold values from -1 to 1
- output_adapter_first: bfloat16 [8192, 32], P('head'), may hold values from -0.0625 to 0.0625
- output_adapter_second: bfloat16 [32, 2560], replicated, may hold values from -1 to 1
- frozen_output_weight: bfloat16 [8192, 2560], P('head', 'ctx'), may hold values from -0.0625 to 0.0625
- output_cotangent: bfloat16 [8192, 2560], P('ctx'), may hold values from -0.1875 to 0.1875
Outputs:
- grad_qa: float32 [1536, 32], replicated
- grad_qb: float32 [32, 12288], P(None, 'head')
- grad_oa: float32 [8192, 32], P('head')
- grad_ob: float32 [32, 2560], P(None, 'ctx')
Inputs may be any that keep to these rules, and one draw needn't show every extreme that they name: For c < 8, each of the 8 groups of one sequence holds block_starts = (c * 64, (15 - c) * 64), every c once per sequence.
All inputs are finite; a program needn't handle non-finite values.
Results may differ from a plain program's by a relative error of at most 0.02.
The roundings to bfloat16 on the way count: a program that leaves them out, or rounds other values in their place, can miss the bound.
Values may be sent and summed in bfloat16 or wider, within the bound.
A program may use at most 128 MiB of HBM per device.

v0:
```python
import jax
import jax.numpy as jnp
from jax import lax
from jax.sharding import PartitionSpec as P

PLAIN_WIDTH = 128
ROTARY_WIDTH = 64
VALUE_WIDTH = 128
KVL = 512
SPAN = 8
ROPE_BASE = 10000.0


def passed_along(value, axis, steps):
    count = lax.axis_size(axis)
    pairs = [(source, (source + steps) % count) for source in range(count)]
    return lax.ppermute(value, axis, pairs)


def rotate(vectors, positions, sign):
    half_width = vectors.shape[-1] // 2
    freq = ROPE_BASE ** (-jnp.arange(half_width, dtype=jnp.float32) * 2.0 / vectors.shape[-1])
    angle = positions.astype(jnp.float32)[..., None] * freq
    angle = angle.reshape(
        positions.shape + (1,) * (vectors.ndim - positions.ndim - 1) + (half_width,)
    )
    cosine = jnp.cos(angle)
    sine = jnp.sin(angle) * sign
    first = vectors[..., :half_width]
    second = vectors[..., half_width:]
    return jnp.concatenate([first * cosine - second * sine, second * cosine + first * sine], -1)


def block_positions(offsets, half_rows):
    steps = jnp.arange(half_rows, dtype=jnp.int32)
    return jnp.concatenate([offsets[0] + steps, offsets[1] + steps])


def expand_block(latent_rows, latent_up_weight, positions):
    kv_up = jnp.dot(
        latent_rows[:, :KVL], latent_up_weight, preferred_element_type=jnp.float32
    ).astype(jnp.bfloat16)
    rope_key = rotate(latent_rows[:, KVL:].astype(jnp.float32), positions, 1.0).astype(jnp.bfloat16)
    return jnp.concatenate([kv_up, rope_key], -1)


def block_scores(query_full, block, head_number):
    split = head_number * (PLAIN_WIDTH + VALUE_WIDTH)
    kv_heads = block[:, :split].reshape(block.shape[0], head_number, PLAIN_WIDTH + VALUE_WIDTH)
    nope_part = jnp.einsum(
        "qhd,khd->hqk",
        query_full[..., :PLAIN_WIDTH],
        kv_heads[..., :PLAIN_WIDTH],
        preferred_element_type=jnp.float32,
    )
    rope_part = jnp.einsum(
        "qhd,kd->hqk",
        query_full[..., PLAIN_WIDTH:],
        block[:, split:],
        preferred_element_type=jnp.float32,
    )
    return nope_part + rope_part


def contract_rows(left, right):
    return lax.dot_general(
        left, right, (((0,), (0,)), ((), ())), preferred_element_type=jnp.float32
    )


def columns_contract(left, right):
    return lax.dot_general(
        left, right, (((1,), (1,)), ((), ())), preferred_element_type=jnp.float32
    )


def body(
    frozen_queries,
    query_latent_rows,
    key_value_latent,
    block_starts,
    latent_up_weight,
    query_adapter_first,
    query_adapter_second,
    output_adapter_first,
    output_adapter_second,
    frozen_output_weight,
    output_cotangent,
):
    token_rows = frozen_queries.shape[0]
    half_rows = token_rows // 2
    per_head_width = PLAIN_WIDTH + ROTARY_WIDTH
    head_number = query_adapter_second.shape[1] // per_head_width
    score_scale = per_head_width ** (-0.5)
    axis_count = lax.axis_size("ctx")
    stride = axis_count // SPAN
    axis_place = lax.axis_index("ctx")
    all_offsets = lax.all_gather(block_starts, "ctx", axis=0, tiled=True)
    own_positions = block_positions(block_starts[0], half_rows)
    query_rank_rows = jnp.dot(
        query_latent_rows, query_adapter_first, preferred_element_type=jnp.float32
    ).astype(jnp.bfloat16)
    query_full = frozen_queries.astype(jnp.float32) + jnp.dot(
        query_rank_rows, query_adapter_second, preferred_element_type=jnp.float32
    )
    query_full = query_full.reshape(token_rows, head_number, per_head_width)
    query_full = jnp.concatenate(
        [query_full[..., :PLAIN_WIDTH], rotate(query_full[..., PLAIN_WIDTH:], own_positions, 1.0)],
        -1,
    ).astype(jnp.bfloat16)

    def prepare(block, positions):
        return expand_block(block, latent_up_weight, positions)

    collected = []

    def take(block, distance):
        source = (axis_place - distance * stride) % axis_count
        source_offsets = lax.dynamic_index_in_dim(all_offsets, source, 0, keepdims=False)
        positions = block_positions(source_offsets, half_rows)
        expanded = prepare(block, positions)
        collected.append((expanded, positions, block_scores(query_full, expanded, head_number)))

    take(key_value_latent, 0)
    moving = key_value_latent
    for hop in range(1, SPAN):
        moving = passed_along(moving, "ctx", stride)
        take(moving, hop)
    kv_all = jnp.concatenate([entry[0] for entry in collected], 0)
    key_positions = jnp.concatenate([entry[1] for entry in collected], 0)
    scores = jnp.concatenate([entry[2] for entry in collected], -1) * score_scale
    causal = key_positions[None, :] <= own_positions[:, None]
    scores = jnp.where(causal[None], scores, -jnp.inf)
    top = jnp.max(scores, -1, keepdims=True)
    expo = jnp.exp(scores - top)
    weights = (expo / jnp.sum(expo, -1, keepdims=True)).astype(jnp.bfloat16)
    split = head_number * (PLAIN_WIDTH + VALUE_WIDTH)
    key_count = kv_all.shape[0]
    kv_heads = kv_all[:, :split].reshape(key_count, head_number, PLAIN_WIDTH + VALUE_WIDTH)
    key_nope = kv_heads[..., :PLAIN_WIDTH]
    values = kv_heads[..., PLAIN_WIDTH:]
    rope_keys = kv_all[:, split:]
    attended_values = jnp.einsum(
        "hqk,khv->qhv", weights, values, preferred_element_type=jnp.float32
    ).astype(jnp.bfloat16)
    attended_flattened = attended_values.reshape(token_rows, head_number * VALUE_WIDTH)
    output_partial_sum = jnp.dot(
        attended_flattened, output_adapter_first, preferred_element_type=jnp.float32
    )
    output_rank_rows = lax.psum(output_partial_sum, "head").astype(jnp.bfloat16)
    output_rank_gradient = columns_contract(output_cotangent, output_adapter_second).astype(
        jnp.bfloat16
    )
    grad_ob = lax.psum_scatter(
        contract_rows(output_rank_rows, output_cotangent), "ctx", scatter_dimension=1, tiled=True
    )
    grad_oa = lax.psum(contract_rows(attended_flattened, output_rank_gradient), "ctx")
    frozen_query_gradient = columns_contract(
        output_cotangent, lax.all_gather(frozen_output_weight, "ctx", axis=1, tiled=True)
    )
    attended_gradient = (
        (frozen_query_gradient + columns_contract(output_rank_gradient, output_adapter_first))
        .astype(jnp.bfloat16)
        .reshape(token_rows, head_number, VALUE_WIDTH)
    )
    d_prob = jnp.einsum(
        "qhv,khv->hqk", attended_gradient, values, preferred_element_type=jnp.float32
    )
    weights_wide = weights.astype(jnp.float32)
    delta = jnp.sum(weights_wide * d_prob, -1, keepdims=True)
    d_score = (weights_wide * (d_prob - delta) * score_scale).astype(jnp.bfloat16)
    dq_nope = jnp.einsum("hqk,khd->qhd", d_score, key_nope, preferred_element_type=jnp.float32)
    dq_rope = jnp.einsum("hqk,kd->qhd", d_score, rope_keys, preferred_element_type=jnp.float32)
    dq_rope = rotate(dq_rope, own_positions, -1.0)
    query_gradient = (
        jnp.concatenate([dq_nope, dq_rope], -1)
        .reshape(token_rows, head_number * per_head_width)
        .astype(jnp.bfloat16)
    )
    qb_term = contract_rows(query_rank_rows, query_gradient)
    query_adapter_gradient = lax.psum(
        columns_contract(query_gradient, query_adapter_second), "head"
    ).astype(jnp.bfloat16)
    qa_term = contract_rows(query_latent_rows, query_adapter_gradient)
    grad_qb, grad_qa = lax.psum((qb_term, qa_term), "ctx")
    return (grad_qa, grad_qb, grad_oa, grad_ob)


def solution(mesh):
    return jax.shard_map(
        body,
        mesh=mesh,
        in_specs=(
            P("ctx", "head"),
            P("ctx", None),
            P("ctx", None),
            P("ctx", None),
            P(None, "head"),
            P(),
            P(None, "head"),
            P("head", None),
            P(),
            P("head", "ctx"),
            P("ctx", None),
        ),
        out_specs=(P(), P(None, "head"), P("head", None), P(None, "ctx")),
        check_vma=False,
    )
```

profile of v0, /device:TPU:1, one launch (start us, length us, event | category | flops | bytes accessed | tf_op | source)
XLA Modules:
  0.0 902.7 jit_solution(16338640068785759681)
XLA Ops:
  7.3 8.5 collective-permute-start
  18.0 1.4 convolution_convert_fusion.7
  24.4 80.7 %all-gather = s32[64,1,2]{2,1,0:T(1,128)} all-gather(s32[1,1,2]{2,1,0:T(1,128)S(1)} %bitcast.209), channel_id=1, replica_groups=mesh['ctx'=64,'head'=8] {'ctx'}, dimensions={0}, use_global_device_ids=true | all-gather | bytes 520 | tf_op jit(solution)/shard_map/all_gather | solution.py:98
  123.5 2.0 fusion.62
  131.0 1.8 convolution_convert_fusion.8
  139.2 1.5 fusion.129
  140.7 1.4 copy.115
  143.5 1.9 concatenate.147
  145.4 1.9 constant_dynamic-update-slice_fusion.7
  148.7 1.9 concatenate.149
  150.6 2.0 constant_dynamic-update-slice_fusion.6
  152.6 1.9 collective-permute-start.1
  154.5 2.0 fusion.60
  156.5 10.0 %collective-permute-done.1 = bf16[128,576]{0,1:T(8,128)(2,1)S(1)} collective-permute-done((bf16[128,576]{0,1:T(8,128)(2,1)}, bf16[128,576]{0,1:T(8,128)(2,1)S(1)}, u32[]{:S(2)}, u32[]{:S(2)}) %collective-permute-start.1) | collective-permute-done | bytes 147488 | tf_op jit(solution)/shard_map/ppermute | solution.py:17
  168.2 1.9 collective-permute-start.2
  170.2 11.2 %collective-permute-done.2 = bf16[128,576]{0,1:T(8,128)(2,1)S(1)} collective-permute-done((bf16[128,576]{0,1:T(8,128)(2,1)S(1)}, bf16[128,576]{0,1:T(8,128)(2,1)S(1)}, u32[]{:S(2)}, u32[]{:S(2)}) %collective-permute-start.2) | collective-permute-done | bytes 147488 | tf_op jit(solution)/shard_map/ppermute | solution.py:17
  183.1 1.9 collective-permute-start.3
  185.0 11.9 %collective-permute-done.3 = bf16[128,576]{0,1:T(8,128)(2,1)S(1)} collective-permute-done((bf16[128,576]{0,1:T(8,128)(2,1)S(1)}, bf16[128,576]{0,1:T(8,128)(2,1)S(1)}, u32[]{:S(2)}, u32[]{:S(2)}) %collective-permute-start.3) | collective-permute-done | bytes 147488 | tf_op jit(solution)/shard_map/ppermute | solution.py:17
  199.9 1.4 copy.119
  201.3 1.4 copy.120
  207.0 1.9 concatenate.151
  208.9 1.9 concatenate.153
  210.7 1.9 concatenate.155
  212.6 1.9 collective-permute-start.4
  214.5 1.9 constant_dynamic-update-slice_fusion.5
  216.5 1.9 constant_dynamic-update-slice_fusion.4
  218.4 1.9 constant_dynamic-update-slice_fusion.3
  220.3 1.9 fusion.54
  222.3 3.1 collective-permute-done.4
  226.0 1.9 collective-permute-start.5
  228.9 10.8 %collective-permute-done.5 = bf16[128,576]{0,1:T(8,128)(2,1)S(1)} collective-permute-done((bf16[128,576]{0,1:T(8,128)(2,1)S(1)}, bf16[128,576]{0,1:T(8,128)(2,1)S(1)}, u32[]{:S(2)}, u32[]{:S(2)}) %collective-permute-start.5) | collective-permute-done | bytes 147488 | tf_op jit(solution)/shard_map/ppermute | solution.py:17
  240.4 1.9 collective-permute-start.6
  243.4 9.6 %collective-permute-done.6 = bf16[128,576]{0,1:T(8,128)(2,1)S(1)} collective-permute-done((bf16[128,576]{0,1:T(8,128)(2,1)S(1)}, bf16[128,576]{0,1:T(8,128)(2,1)S(1)}, u32[]{:S(2)}, u32[]{:S(2)}) %collective-permute-start.6) | collective-permute-done | bytes 147488 | tf_op jit(solution)/shard_map/ppermute | solution.py:17
  262.6 2.5 slice.337
  265.3 1.5 copy.186
  269.5 1.6 fusion.178
  271.0 1.9 fusion.188
  273.4 1.4 copy-done.18
  277.3 3.3 fusion.197
  280.9 2.7 fusion.16
  283.6 6.7 fusion.42
  290.4 7.4 fusion.43
  300.0 50.8 %all-reduce.2 = (bf16[128,32]{0,1:T(8,128)(2,1)S(1)}, bf16[128,32]{0,1:T(8,128)(2,1)S(1)}) all-reduce(f32[128,32]{0,1:T(8,128)S(1)} %fusion.200, f32[128,32]{0,1:T(8,128)} %fusion.201), channel_id=1, replica_groups=mesh['ctx'=64,'head'=8] {'head'}, use_global_device_ids=true, to_apply=%region_3.4 | all-reduce | flops 8192 | bytes 49152 | tf_op jit(solution)/shard_map/psum | solution.py:181
  354.6 535.1 %all-reduce.5.cloned.1.call-done = (f32[1536,32]{0,1:T(8,128)}, f32[32,1536]{1,0:T(8,128)}, f32[1024,32]{0,1:T(8,128)}, f32[32,2560]{1,0:T(8,128)}) async-done(((f32[1536,32]{0,1:T(8,128)}, f32[32,1536]{1,0:T(8,128)}, f32[1024,32]{0,1:T(8,128)}, f32[32,2560]{1,0:T(8,128)}), (f32[1536,32]{0,1:T(8,128)}, f32[32,1536]{1,0:T(8,128)}, f32[1024,32]{0,1:T(8,128)}, ...) | async-done | bytes 851984 | tf_op jit(solution)/shard_map/psum | solution.py:185
  889.6 1.4 constant_dynamic-slice_fusion.8
  891.1 1.6 copy.245
  892.7 1.6 copy.246
  894.3 1.6 copy.247
  (281 shorter events, 74.0 us)
Async XLA Ops:
  7.2 10.8 %copy-start = (bf16[512,2048]{1,0:T(8,128)(2,1)S(1)}, bf16[512,2048]{1,0:T(8,128)(2,1)}, u32[]{:S(2)}) copy-start(bf16[512,2048]{1,0:T(8,128)(2,1)} %param.15) | copy-start | bytes 6291460
  7.2 13.1 %copy-start.19 = (bf16[128,1536]{1,0:T(8,128)(2,1)S(1)}, bf16[128,1536]{1,0:T(8,128)(2,1)}, u32[]{:S(2)}) copy-start(bf16[128,1536]{1,0:T(8,128)(2,1)} %param.12) | copy-start | bytes 1179652
  7.2 14.0 %copy-start.21 = (bf16[128,1536]{1,0:T(8,128)(2,1)S(1)}, bf16[128,1536]{1,0:T(8,128)(2,1)}, u32[]{:S(2)}) copy-start(bf16[128,1536]{1,0:T(8,128)(2,1)} %param.11) | copy-start | bytes 1179652
  7.2 16.6 %copy-start.62 = (s32[1,2]{1,0:T(1,128)S(1)}, s32[1,2]{1,0:T(1,128)}, u32[]{:S(2)}) copy-start(s32[1,2]{1,0:T(1,128)} %param.14) | copy-start | bytes 28
  7.2 270.1 %all-gather.3.cloned.1.call-start = ((), (), s32[]{:S(2)}) async-start(), calls=%async_computation | async-start | bytes 5324800 | tf_op jit(solution)/shard_map/all_gather | solution.py:159
  7.3 128.1 %collective-permute-start = (bf16[128,576]{0,1:T(8,128)(2,1)}, bf16[128,576]{0,1:T(8,128)(2,1)}, u32[]{:S(2)}, u32[]{:S(2)}) collective-permute-start(bf16[128,576]{0,1:T(8,128)(2,1)} %param.13), channel_id=1, source_target_pairs={{0,64},{8,72},{16,80},{24,88},{32,96},{40,104},{48,112},{56,120},{... | collective-permute-start | bytes 442376 | tf_op jit(solution)/shard_map/ppermute | solution.py:17
  15.8 873.8 %all-reduce.5.cloned.1.call-start = ((), (), s32[]{:S(2)}) async-start(), calls=%async_computation.1 | async-start | bytes 1703936 | tf_op jit(solution)/shard_map/psum | solution.py:185
  16.0 4.3 copy-start.28
  16.0 5.1 copy-start.22
  18.0 113.1 %copy-start.2 = (bf16[128,2560]{1,0:T(8,128)(2,1)S(1)}, bf16[128,2560]{1,0:T(8,128)(2,1)}, u32[]{:S(2)}) copy-start(bf16[128,2560]{1,0:T(8,128)(2,1)} %param.21) | copy-start | bytes 1966084
  109.0 19.7 %copy-start.70 = (s32[64]{0:T(128)}, s32[64]{0:T(128)S(1)}, u32[]{:S(2)}) copy-start(s32[64]{0:T(128)S(1)} %iota_add_fusion.14) | copy-start | bytes 772
  109.6 19.1 %copy-start.71 = (s32[64]{0:T(128)}, s32[64]{0:T(128)S(1)}, u32[]{:S(2)}) copy-start(s32[64]{0:T(128)S(1)} %iota_add_fusion.15) | copy-start | bytes 772
  110.9 17.8 %copy-start.78 = (s32[64]{0:T(128)}, s32[64]{0:T(128)S(1)}, u32[]{:S(2)}) copy-start(s32[64]{0:T(128)S(1)} %iota_add_fusion.2) | copy-start | bytes 772
  111.5 17.2 %copy-start.79 = (s32[64]{0:T(128)}, s32[64]{0:T(128)S(1)}, u32[]{:S(2)}) copy-start(s32[64]{0:T(128)S(1)} %iota_add_fusion.3) | copy-start | bytes 772
  112.8 15.9 %copy-start.72 = (s32[64]{0:T(128)}, s32[64]{0:T(128)S(1)}, u32[]{:S(2)}) copy-start(s32[64]{0:T(128)S(1)} %iota_add_fusion.6) | copy-start | bytes 772
  113.5 15.3 %copy-start.73 = (s32[64]{0:T(128)}, s32[64]{0:T(128)S(1)}, u32[]{:S(2)}) copy-start(s32[64]{0:T(128)S(1)} %iota_add_fusion.7) | copy-start | bytes 772
  114.7 14.0 %copy-start.74 = (s32[64]{0:T(128)}, s32[64]{0:T(128)S(1)}, u32[]{:S(2)}) copy-start(s32[64]{0:T(128)S(1)} %iota_add_fusion.4) | copy-start | bytes 772
  115.4 13.4 %copy-start.75 = (s32[64]{0:T(128)}, s32[64]{0:T(128)S(1)}, u32[]{:S(2)}) copy-start(s32[64]{0:T(128)S(1)} %iota_add_fusion.5) | copy-start | bytes 772
  130.2 9.0 %copy-start.26 = (f32[128,64]{0,1:T(8,128)S(1)}, f32[128,64]{0,1:T(8,128)}, u32[]{:S(2)}) copy-start(f32[128,64]{0,1:T(8,128)} %slice_convert_fusion.8) | copy-start | bytes 98308
  130.2 9.0 %copy-start.68 = (f32[128]{0:T(128)S(1)}, f32[128]{0:T(128)}, u32[]{:S(2)}) copy-start(f32[128]{0:T(128)} %get-tuple-element.77) | copy-start | bytes 1540
  130.2 9.0 %copy-start.69 = (f32[128]{0:T(128)S(1)}, f32[128]{0:T(128)}, u32[]{:S(2)}) copy-start(f32[128]{0:T(128)} %get-tuple-element.78) | copy-start | bytes 1540
  140.7 26.3 %copy-start.32 = (bf16[128,32]{0,1:T(8,128)(2,1)}, bf16[128,32]{0,1:T(8,128)(2,1)S(1)}, u32[]{:S(2)}) copy-start(bf16[128,32]{0,1:T(8,128)(2,1)S(1)} %get-tuple-element.30) | copy-start | bytes 24580
  140.7 26.3 %copy-start.34 = (bf16[128,32]{0,1:T(8,128)(2,1)}, bf16[128,32]{0,1:T(8,128)(2,1)S(1)}, u32[]{:S(2)}) copy-start(bf16[128,32]{0,1:T(8,128)(2,1)S(1)} %get-tuple-element.31) | copy-start | bytes 24580
  152.6 13.9 %collective-permute-start.1 = (bf16[128,576]{0,1:T(8,128)(2,1)}, bf16[128,576]{0,1:T(8,128)(2,1)S(1)}, u32[]{:S(2)}, u32[]{:S(2)}) collective-permute-start(bf16[128,576]{0,1:T(8,128)(2,1)} %collective-permute-done), channel_id=1, source_target_pairs={{0,64},{8,72},{16,80},{24,88},{32,96},{40,104},{48,112},{56,120},{... | collective-permute-start | bytes 442376 | tf_op jit(solution)/shard_map/ppermute | solution.py:17
  167.0 16.1 %copy-start.5 = (bf16[128,2048]{1,0:T(8,128)(2,1)}, bf16[128,2048]{1,0:T(8,128)(2,1)S(1)}, u32[]{:S(2)}) copy-start(bf16[128,2048]{1,0:T(8,128)(2,1)S(1)} %convolution_convert_fusion.5) | copy-start | bytes 1572868
  168.2 13.1 %collective-permute-start.2 = (bf16[128,576]{0,1:T(8,128)(2,1)S(1)}, bf16[128,576]{0,1:T(8,128)(2,1)S(1)}, u32[]{:S(2)}, u32[]{:S(2)}) collective-permute-start(bf16[128,576]{0,1:T(8,128)(2,1)S(1)} %collective-permute-done.1), channel_id=1, source_target_pairs={{0,64},{8,72},{16,80},{24,88},{32,96},{40,104},{48,112},{56,120},{... | collective-permute-start | bytes 442376 | tf_op jit(solution)/shard_map/ppermute | solution.py:17
  181.8 17.1 %copy-start.60 = (f32[32]{0:T(128)S(1)}, f32[32]{0:T(128)}, u32[]{:S(2)}) copy-start(f32[32]{0:T(128)} %multiply_power_fusion) | copy-start | bytes 388
  181.8 17.1 %copy-start.66 = (f32[128]{0:T(128)S(1)}, f32[128]{0:T(128)}, u32[]{:S(2)}) copy-start(f32[128]{0:T(128)} %get-tuple-element.79) | copy-start | bytes 1540
  181.8 17.1 %copy-start.67 = (f32[128]{0:T(128)S(1)}, f32[128]{0:T(128)}, u32[]{:S(2)}) copy-start(f32[128]{0:T(128)} %get-tuple-element.80) | copy-start | bytes 1540
  181.9 17.1 %copy-start.77 = (f32[128]{0:T(128)S(1)}, f32[128]{0:T(128)}, u32[]{:S(2)}) copy-start(f32[128]{0:T(128)} %add_convert_fusion.6) | copy-start | bytes 1540
  183.1 13.8 %collective-permute-start.3 = (bf16[128,576]{0,1:T(8,128)(2,1)S(1)}, bf16[128,576]{0,1:T(8,128)(2,1)S(1)}, u32[]{:S(2)}, u32[]{:S(2)}) collective-permute-start(bf16[128,576]{0,1:T(8,128)(2,1)S(1)} %collective-permute-done.2), channel_id=1, source_target_pairs={{0,64},{8,72},{16,80},{24,88},{32,96},{40,104},{48,112},{56,120},{... | collective-permute-start | bytes 442376 | tf_op jit(solution)/shard_map/ppermute | solution.py:17
  199.9 25.9 %copy-start.38 = (bf16[128,32]{0,1:T(8,128)(2,1)}, bf16[128,32]{0,1:T(8,128)(2,1)S(1)}, u32[]{:S(2)}) copy-start(bf16[128,32]{0,1:T(8,128)(2,1)S(1)} %get-tuple-element.24) | copy-start | bytes 24580
  199.9 25.9 %copy-start.40 = (bf16[128,32]{0,1:T(8,128)(2,1)}, bf16[128,32]{0,1:T(8,128)(2,1)S(1)}, u32[]{:S(2)}) copy-start(bf16[128,32]{0,1:T(8,128)(2,1)S(1)} %get-tuple-element.25) | copy-start | bytes 24580
  212.6 12.7 %collective-permute-start.4 = (bf16[128,576]{0,1:T(8,128)(2,1)}, bf16[128,576]{0,1:T(8,128)(2,1)S(1)}, u32[]{:S(2)}, u32[]{:S(2)}) collective-permute-start(bf16[128,576]{0,1:T(8,128)(2,1)} %copy-done.25), channel_id=1, source_target_pairs={{0,64},{8,72},{16,80},{24,88},{32,96},{40,104},{48,112},{56,120},{... | collective-permute-start | bytes 442376 | tf_op jit(solution)/shard_map/ppermute | solution.py:17
  225.8 17.6 %copy-start.4 = (bf16[128,2048]{1,0:T(8,128)(2,1)}, bf16[128,2048]{1,0:T(8,128)(2,1)S(1)}, u32[]{:S(2)}) copy-start(bf16[128,2048]{1,0:T(8,128)(2,1)S(1)} %convolution_convert_fusion.2) | copy-start | bytes 1572868
  226.0 13.8 %collective-permute-start.5 = (bf16[128,576]{0,1:T(8,128)(2,1)S(1)}, bf16[128,576]{0,1:T(8,128)(2,1)S(1)}, u32[]{:S(2)}, u32[]{:S(2)}) collective-permute-start(bf16[128,576]{0,1:T(8,128)(2,1)S(1)} %collective-permute-done.4), channel_id=1, source_target_pairs={{0,64},{8,72},{16,80},{24,88},{32,96},{40,104},{48,112},{56,120},{... | collective-permute-start | bytes 442376 | tf_op jit(solution)/shard_map/ppermute | solution.py:17
  240.2 14.2 %copy-start.61 = (f32[32]{0:T(128)S(1)}, f32[32]{0:T(128)}, u32[]{:S(2)}) copy-start(f32[32]{0:T(128)} %multiply_power_fusion) | copy-start | bytes 388
  240.2 14.2 %copy-start.63 = (f32[128]{0:T(128)S(1)}, f32[128]{0:T(128)}, u32[]{:S(2)}) copy-start(f32[128]{0:T(128)} %get-tuple-element.10) | copy-start | bytes 1540
  240.3 14.2 %copy-start.64 = (f32[128]{0:T(128)S(1)}, f32[128]{0:T(128)}, u32[]{:S(2)}) copy-start(f32[128]{0:T(128)} %get-tuple-element.81) | copy-start | bytes 1540
  240.3 14.2 %copy-start.65 = (f32[128]{0:T(128)S(1)}, f32[128]{0:T(128)}, u32[]{:S(2)}) copy-start(f32[128]{0:T(128)} %get-tuple-element.82) | copy-start | bytes 1540
  240.3 14.2 %copy-start.76 = (f32[128]{0:T(128)S(1)}, f32[128]{0:T(128)}, u32[]{:S(2)}) copy-start(f32[128]{0:T(128)} %add_convert_fusion.9) | copy-start | bytes 1540
  240.4 12.6 %collective-permute-start.6 = (bf16[128,576]{0,1:T(8,128)(2,1)S(1)}, bf16[128,576]{0,1:T(8,128)(2,1)S(1)}, u32[]{:S(2)}, u32[]{:S(2)}) collective-permute-start(bf16[128,576]{0,1:T(8,128)(2,1)S(1)} %collective-permute-done.5), channel_id=1, source_target_pairs={{0,64},{8,72},{16,80},{24,88},{32,96},{40,104},{48,112},{56,120},{... | collective-permute-start | bytes 442376 | tf_op jit(solution)/shard_map/ppermute | solution.py:17
  273.0 3.5 copy-start.31
  290.4 7.5 copy-start.58
  290.4 8.5 copy-start.23
  290.4 8.7 copy-start.30
  290.4 60.4 %copy-start.20 = (bf16[128,1536]{1,0:T(8,128)(2,1)S(1)}, bf16[128,1536]{1,0:T(8,128)(2,1)}, u32[]{:S(2)}) copy-start(bf16[128,1536]{1,0:T(8,128)(2,1)} %param.12) | copy-start | bytes 1179652
  290.4 605.5 %copy-start.1 = (bf16[512,2048]{1,0:T(8,128)(2,1)S(1)}, bf16[512,2048]{1,0:T(8,128)(2,1)}, u32[]{:S(2)}) copy-start(bf16[512,2048]{1,0:T(8,128)(2,1)} %param.15) | copy-start | bytes 6291460
  (41 other events, 68.4 us)
Sparse Core Ops, SparseCore 0:
  15.9 122.1 all-gather.2
  352.8 536.8 all-reduce.4
where the time goes:
time: 905 us; the launch traced here: 903 us
  waiting for transfers between devices  592 us (65%)
  blocking collectives  131 us (14%)
  local copies, waits for them, and re-layouts  66.2 us (7%)
  matrix products  47 us (5%)
  other arithmetic  30 us (3%)
  starting transfers between devices  20.1 us (2%)
  between operations  16.3 us (2%)
    psum x1, waiting for transfers between devices, body(): grad_qb, grad_qa = lax.psum((qb_term, qa_term), 'ctx')  535 us
    all_gather x1, blocking collectives, body(): all_offsets = lax.all_gather(block_starts, 'ctx', axis=0, tiled=True)  80.7 us
    ppermute x7, waiting for transfers between devices, passed_along(): return lax.ppermute(value, axis, pairs)  56.6 us
    psum x1, blocking collectives, body(): lax.psum(columns_contract(query_gradient, query_adapter_second), 'head')  50.8 us
    unnamed x181, local copies, waits for them, and re-layouts  26.2 us
    ppermute x7, starting transfers between devices, passed_along(): return lax.ppermute(value, axis, pairs)  20 us
  transfers between devices with their start and end apart: 9, of which 7 were waited for; matrix products, arithmetic and copies ran while one was open for 12% of the time, Pallas kernels for 0%

commit v1 on v0

--- a/solution.py
+++ b/solution.py
@@ -178,9 +178,11 @@
         .astype(jnp.bfloat16)
     )
     qb_term = contract_rows(query_rank_rows, query_gradient)
-    query_adapter_gradient = lax.psum(
-        columns_contract(query_gradient, query_adapter_second), "head"
-    ).astype(jnp.bfloat16)
+    query_adapter_gradient = (
+        lax.all_gather(columns_contract(query_gradient, query_adapter_second), "head")
+        .sum(axis=0)
+        .astype(jnp.bfloat16)
+    )
     qa_term = contract_rows(query_latent_rows, query_adapter_gradient)
     grad_qb, grad_qa = lax.psum((qb_term, qa_term), "ctx")
     return (grad_qa, grad_qb, grad_oa, grad_ob)

time: 905 us -> 938 us (1.036)
  blocking collectives: 131 us -> 168 us
    all_gather x0 -> x1, blocking collectives: none -> 37.4 us  [body(): lax.all_gather(columns_contract(query_gradient, query_adapter_second), 'h...]
    unnamed x181 -> x182, local copies, waits for them, and re-layouts: 26.2 us -> 26.2 us
  transfers between devices with their start and end apart: 9 -> 9, of which waited for: 7 -> 7; matrix products, arithmetic and copies ran while one was open for 12% -> 11% of each run, Pallas kernels for 0% -> 0%
where the time goes in v1:
time: 938 us; the launch traced here: 936 us
  waiting for transfers between devices  591 us (63%)
  blocking collectives  168 us (18%)
  local copies, waits for them, and re-layouts  66.1 us (7%)
  matrix products  45.6 us (5%)
  other arithmetic  28.9 us (3%)
  starting transfers between devices  20.3 us (2%)
  between operations  16.4 us (2%)
    psum x1, waiting for transfers between devices, body(): grad_qb, grad_qa = lax.psum((qb_term, qa_term), 'ctx')  535 us
    all_gather x1, blocking collectives, body(): all_offsets = lax.all_gather(block_starts, 'ctx', axis=0, tiled=True)  80.7 us
    ppermute x7, waiting for transfers between devices, passed_along(): return lax.ppermute(value, axis, pairs)  55.7 us
    psum x1, blocking collectives, body(): output_rank_rows = lax.psum(output_partial_sum, 'head').astype(jnp.bfloat16)  50.2 us
    all_gather x1, blocking collectives, body(): lax.all_gather(columns_contract(query_gradient, query_adapter_second), 'h...  37.4 us
    unnamed x182, local copies, waits for them, and re-layouts  26.2 us
    ppermute x7, starting transfers between devices, passed_along(): return lax.ppermute(value, axis, pairs)  20.2 us
  transfers between devices with their start and end apart: 9, of which 7 were waited for; matrix products, arithmetic and copies ran while one was open for 11% of the time, Pallas kernels for 0%

profile of v1, /device:TPU:1, one launch (start us, length us, event | category | flops | bytes accessed | tf_op | source)
XLA Modules:
  0.0 936.4 jit_solution(12284490339084800362)
XLA Ops:
  7.3 8.5 collective-permute-start
  18.0 1.4 convolution_convert_fusion.7
  24.4 80.7 %all-gather.1 = s32[64,1,2]{2,1,0:T(1,128)} all-gather(s32[1,1,2]{2,1,0:T(1,128)S(1)} %bitcast.215), channel_id=1, replica_groups=mesh['ctx'=64,'head'=8] {'ctx'}, dimensions={0}, use_global_device_ids=true | all-gather | bytes 520 | tf_op jit(solution)/shard_map/all_gather | solution.py:98
  123.6 2.0 fusion.62
  130.9 1.8 convolution_convert_fusion.8
  139.0 1.5 fusion.129
  140.5 1.4 copy.115
  143.4 1.9 concatenate.147
  145.2 1.9 constant_dynamic-update-slice_fusion.7
  148.6 1.9 concatenate.149
  150.4 1.9 constant_dynamic-update-slice_fusion.6
  152.4 1.9 collective-permute-start.1
  154.3 2.0 fusion.60
  156.2 10.1 %collective-permute-done.1 = bf16[128,576]{0,1:T(8,128)(2,1)S(1)} collective-permute-done((bf16[128,576]{0,1:T(8,128)(2,1)}, bf16[128,576]{0,1:T(8,128)(2,1)S(1)}, u32[]{:S(2)}, u32[]{:S(2)}) %collective-permute-start.1) | collective-permute-done | bytes 147488 | tf_op jit(solution)/shard_map/ppermute | solution.py:17
  168.0 1.9 collective-permute-start.2
  169.9 12.2 %collective-permute-done.2 = bf16[128,576]{0,1:T(8,128)(2,1)S(1)} collective-permute-done((bf16[128,576]{0,1:T(8,128)(2,1)S(1)}, bf16[128,576]{0,1:T(8,128)(2,1)S(1)}, u32[]{:S(2)}, u32[]{:S(2)}) %collective-permute-start.2) | collective-permute-done | bytes 147488 | tf_op jit(solution)/shard_map/ppermute | solution.py:17
  183.9 1.9 collective-permute-start.3
  185.8 10.5 %collective-permute-done.3 = bf16[128,576]{0,1:T(8,128)(2,1)S(1)} collective-permute-done((bf16[128,576]{0,1:T(8,128)(2,1)S(1)}, bf16[128,576]{0,1:T(8,128)(2,1)S(1)}, u32[]{:S(2)}, u32[]{:S(2)}) %collective-permute-start.3) | collective-permute-done | bytes 147488 | tf_op jit(solution)/shard_map/ppermute | solution.py:17
  199.4 1.4 copy.119
  206.5 1.9 concatenate.151
  208.4 1.9 concatenate.153
  210.3 1.9 concatenate.155
  212.2 1.9 collective-permute-start.4
  214.1 1.9 constant_dynamic-update-slice_fusion.5
  216.1 2.0 constant_dynamic-update-slice_fusion.4
  218.0 1.9 constant_dynamic-update-slice_fusion.3
  219.9 1.9 fusion.54
  221.9 3.0 collective-permute-done.4
  225.5 1.9 collective-permute-start.5
  228.5 10.4 %collective-permute-done.5 = bf16[128,576]{0,1:T(8,128)(2,1)S(1)} collective-permute-done((bf16[128,576]{0,1:T(8,128)(2,1)S(1)}, bf16[128,576]{0,1:T(8,128)(2,1)S(1)}, u32[]{:S(2)}, u32[]{:S(2)}) %collective-permute-start.5) | collective-permute-done | bytes 147488 | tf_op jit(solution)/shard_map/ppermute | solution.py:17
  239.6 2.1 collective-permute-start.6
  242.8 9.4 %collective-permute-done.6 = bf16[128,576]{0,1:T(8,128)(2,1)S(1)} collective-permute-done((bf16[128,576]{0,1:T(8,128)(2,1)S(1)}, bf16[128,576]{0,1:T(8,128)(2,1)S(1)}, u32[]{:S(2)}, u32[]{:S(2)}) %collective-permute-start.6) | collective-permute-done | bytes 147488 | tf_op jit(solution)/shard_map/ppermute | solution.py:17
  261.6 2.5 slice.337
  264.2 1.5 copy.186
  268.4 1.6 fusion.178
  270.0 1.9 fusion.188
  272.3 1.4 copy-done.18
  274.8 50.2 %psum.31 = bf16[128,32]{0,1:T(8,128)(2,1)S(1)} all-reduce(f32[128,32]{0,1:T(8,128)S(1)} %fusion.201), channel_id=1, replica_groups=mesh['ctx'=64,'head'=8] {'head'}, use_global_device_ids=true, to_apply=%region_7.8 | all-reduce | flops 4096 | bytes 24576 | tf_op jit(solution)/shard_map/psum | solution.py:150
  326.8 3.3 fusion.197
  330.4 2.7 fusion.16
  333.1 6.0 fusion.42
  339.2 7.4 fusion.43
  347.8 37.4 %all-gather = f32[1024,32]{0,1:T(8,128)S(1)} all-gather(f32[128,32]{0,1:T(8,128)S(1)} %fusion.200), channel_id=2, replica_groups=mesh['ctx'=64,'head'=8] {'head'}, dimensions={0}, use_global_device_ids=true | all-gather | bytes 147456 | tf_op jit(solution)/shard_map/all_gather | solution.py:182
  388.1 535.2 %all-reduce.4.cloned.1.call-done = (f32[1536,32]{0,1:T(8,128)}, f32[32,1536]{1,0:T(8,128)}, f32[1024,32]{0,1:T(8,128)}, f32[32,2560]{1,0:T(8,128)}) async-done(((f32[1536,32]{0,1:T(8,128)}, f32[32,1536]{1,0:T(8,128)}, f32[1024,32]{0,1:T(8,128)}, f32[32,2560]{1,0:T(8,128)}), (f32[1536,32]{0,1:T(8,128)}, f32[32,1536]{1,0:T(8,128)}, f32[1024,32]{0,1:T(8,128)}, ...) | async-done | bytes 851984 | tf_op jit(solution)/shard_map/psum | solution.py:187
  923.3 1.4 constant_dynamic-slice_fusion.8
  924.7 1.6 copy.246
  926.3 1.6 copy.247
  928.0 1.6 copy.248
  (284 shorter events, 73.6 us)
Async XLA Ops:
  7.2 10.8 %copy-start = (bf16[512,2048]{1,0:T(8,128)(2,1)S(1)}, bf16[512,2048]{1,0:T(8,128)(2,1)}, u32[]{:S(2)}) copy-start(bf16[512,2048]{1,0:T(8,128)(2,1)} %param.15) | copy-start | bytes 6291460
  7.2 13.1 %copy-start.19 = (bf16[128,1536]{1,0:T(8,128)(2,1)S(1)}, bf16[128,1536]{1,0:T(8,128)(2,1)}, u32[]{:S(2)}) copy-start(bf16[128,1536]{1,0:T(8,128)(2,1)} %param.12) | copy-start | bytes 1179652
  7.2 13.9 %copy-start.21 = (bf16[128,1536]{1,0:T(8,128)(2,1)S(1)}, bf16[128,1536]{1,0:T(8,128)(2,1)}, u32[]{:S(2)}) copy-start(bf16[128,1536]{1,0:T(8,128)(2,1)} %param.11) | copy-start | bytes 1179652
  7.2 16.5 %copy-start.62 = (s32[1,2]{1,0:T(1,128)S(1)}, s32[1,2]{1,0:T(1,128)}, u32[]{:S(2)}) copy-start(s32[1,2]{1,0:T(1,128)} %param.14) | copy-start | bytes 28
  7.2 319.5 %all-gather.4.cloned.1.call-start = ((), (), s32[]{:S(2)}) async-start(), calls=%async_computation | async-start | bytes 5324800 | tf_op jit(solution)/shard_map/all_gather | solution.py:159
  7.3 128.0 %collective-permute-start = (bf16[128,576]{0,1:T(8,128)(2,1)}, bf16[128,576]{0,1:T(8,128)(2,1)}, u32[]{:S(2)}, u32[]{:S(2)}) collective-permute-start(bf16[128,576]{0,1:T(8,128)(2,1)} %param.13), channel_id=1, source_target_pairs={{0,64},{8,72},{16,80},{24,88},{32,96},{40,104},{48,112},{56,120},{... | collective-permute-start | bytes 442376 | tf_op jit(solution)/shard_map/ppermute | solution.py:17
  15.8 907.5 %all-reduce.4.cloned.1.call-start = ((), (), s32[]{:S(2)}) async-start(), calls=%async_computation.1 | async-start | bytes 1703936 | tf_op jit(solution)/shard_map/psum | solution.py:187
  16.0 4.3 copy-start.28
  16.0 5.1 copy-start.22
  18.0 113.0 %copy-start.2 = (bf16[128,2560]{1,0:T(8,128)(2,1)S(1)}, bf16[128,2560]{1,0:T(8,128)(2,1)}, u32[]{:S(2)}) copy-start(bf16[128,2560]{1,0:T(8,128)(2,1)} %param.21) | copy-start | bytes 1966084
  108.9 19.7 %copy-start.70 = (s32[64]{0:T(128)}, s32[64]{0:T(128)S(1)}, u32[]{:S(2)}) copy-start(s32[64]{0:T(128)S(1)} %iota_add_fusion.14) | copy-start | bytes 772
  109.5 19.1 %copy-start.71 = (s32[64]{0:T(128)}, s32[64]{0:T(128)S(1)}, u32[]{:S(2)}) copy-start(s32[64]{0:T(128)S(1)} %iota_add_fusion.15) | copy-start | bytes 772
  110.8 17.8 %copy-start.78 = (s32[64]{0:T(128)}, s32[64]{0:T(128)S(1)}, u32[]{:S(2)}) copy-start(s32[64]{0:T(128)S(1)} %iota_add_fusion.2) | copy-start | bytes 772
  111.5 17.1 %copy-start.79 = (s32[64]{0:T(128)}, s32[64]{0:T(128)S(1)}, u32[]{:S(2)}) copy-start(s32[64]{0:T(128)S(1)} %iota_add_fusion.3) | copy-start | bytes 772
  112.8 15.9 %copy-start.72 = (s32[64]{0:T(128)}, s32[64]{0:T(128)S(1)}, u32[]{:S(2)}) copy-start(s32[64]{0:T(128)S(1)} %iota_add_fusion.6) | copy-start | bytes 772
  113.4 15.2 %copy-start.73 = (s32[64]{0:T(128)}, s32[64]{0:T(128)S(1)}, u32[]{:S(2)}) copy-start(s32[64]{0:T(128)S(1)} %iota_add_fusion.7) | copy-start | bytes 772
  114.7 14.0 %copy-start.74 = (s32[64]{0:T(128)}, s32[64]{0:T(128)S(1)}, u32[]{:S(2)}) copy-start(s32[64]{0:T(128)S(1)} %iota_add_fusion.4) | copy-start | bytes 772
  115.3 13.3 %copy-start.75 = (s32[64]{0:T(128)}, s32[64]{0:T(128)S(1)}, u32[]{:S(2)}) copy-start(s32[64]{0:T(128)S(1)} %iota_add_fusion.5) | copy-start | bytes 772
  130.1 9.0 copy-start.26
  130.1 9.0 copy-start.68
  130.1 9.0 copy-start.69
  140.5 26.2 %copy-start.32 = (bf16[128,32]{0,1:T(8,128)(2,1)}, bf16[128,32]{0,1:T(8,128)(2,1)S(1)}, u32[]{:S(2)}) copy-start(bf16[128,32]{0,1:T(8,128)(2,1)S(1)} %get-tuple-element.28) | copy-start | bytes 24580
  140.5 26.2 %copy-start.34 = (bf16[128,32]{0,1:T(8,128)(2,1)}, bf16[128,32]{0,1:T(8,128)(2,1)S(1)}, u32[]{:S(2)}) copy-start(bf16[128,32]{0,1:T(8,128)(2,1)S(1)} %get-tuple-element.29) | copy-start | bytes 24580
  152.4 13.9 %collective-permute-start.1 = (bf16[128,576]{0,1:T(8,128)(2,1)}, bf16[128,576]{0,1:T(8,128)(2,1)S(1)}, u32[]{:S(2)}, u32[]{:S(2)}) collective-permute-start(bf16[128,576]{0,1:T(8,128)(2,1)} %collective-permute-done), channel_id=1, source_target_pairs={{0,64},{8,72},{16,80},{24,88},{32,96},{40,104},{48,112},{56,120},{... | collective-permute-start | bytes 442376 | tf_op jit(solution)/shard_map/ppermute | solution.py:17
  166.8 17.1 %copy-start.5 = (bf16[128,2048]{1,0:T(8,128)(2,1)}, bf16[128,2048]{1,0:T(8,128)(2,1)S(1)}, u32[]{:S(2)}) copy-start(bf16[128,2048]{1,0:T(8,128)(2,1)S(1)} %convolution_convert_fusion.5) | copy-start | bytes 1572868
  168.0 14.2 %collective-permute-start.2 = (bf16[128,576]{0,1:T(8,128)(2,1)S(1)}, bf16[128,576]{0,1:T(8,128)(2,1)S(1)}, u32[]{:S(2)}, u32[]{:S(2)}) collective-permute-start(bf16[128,576]{0,1:T(8,128)(2,1)S(1)} %collective-permute-done.1), channel_id=1, source_target_pairs={{0,64},{8,72},{16,80},{24,88},{32,96},{40,104},{48,112},{56,120},{... | collective-permute-start | bytes 442376 | tf_op jit(solution)/shard_map/ppermute | solution.py:17
  182.7 15.8 %copy-start.60 = (f32[32]{0:T(128)S(1)}, f32[32]{0:T(128)}, u32[]{:S(2)}) copy-start(f32[32]{0:T(128)} %multiply_power_fusion) | copy-start | bytes 388
  182.7 15.8 %copy-start.66 = (f32[128]{0:T(128)S(1)}, f32[128]{0:T(128)}, u32[]{:S(2)}) copy-start(f32[128]{0:T(128)} %get-tuple-element.77) | copy-start | bytes 1540
  182.7 15.8 %copy-start.67 = (f32[128]{0:T(128)S(1)}, f32[128]{0:T(128)}, u32[]{:S(2)}) copy-start(f32[128]{0:T(128)} %get-tuple-element.78) | copy-start | bytes 1540
  182.7 15.8 %copy-start.77 = (f32[128]{0:T(128)S(1)}, f32[128]{0:T(128)}, u32[]{:S(2)}) copy-start(f32[128]{0:T(128)} %add_convert_fusion.6) | copy-start | bytes 1540
  183.9 12.5 %collective-permute-start.3 = (bf16[128,576]{0,1:T(8,128)(2,1)S(1)}, bf16[128,576]{0,1:T(8,128)(2,1)S(1)}, u32[]{:S(2)}, u32[]{:S(2)}) collective-permute-start(bf16[128,576]{0,1:T(8,128)(2,1)S(1)} %collective-permute-done.2), channel_id=1, source_target_pairs={{0,64},{8,72},{16,80},{24,88},{32,96},{40,104},{48,112},{56,120},{... | collective-permute-start | bytes 442376 | tf_op jit(solution)/shard_map/ppermute | solution.py:17
  199.4 25.9 %copy-start.38 = (bf16[128,32]{0,1:T(8,128)(2,1)}, bf16[128,32]{0,1:T(8,128)(2,1)S(1)}, u32[]{:S(2)}) copy-start(bf16[128,32]{0,1:T(8,128)(2,1)S(1)} %get-tuple-element.22) | copy-start | bytes 24580
  199.4 26.0 %copy-start.40 = (bf16[128,32]{0,1:T(8,128)(2,1)}, bf16[128,32]{0,1:T(8,128)(2,1)S(1)}, u32[]{:S(2)}) copy-start(bf16[128,32]{0,1:T(8,128)(2,1)S(1)} %get-tuple-element.23) | copy-start | bytes 24580
  212.2 12.7 %collective-permute-start.4 = (bf16[128,576]{0,1:T(8,128)(2,1)}, bf16[128,576]{0,1:T(8,128)(2,1)S(1)}, u32[]{:S(2)}, u32[]{:S(2)}) collective-permute-start(bf16[128,576]{0,1:T(8,128)(2,1)} %copy-done.25), channel_id=1, source_target_pairs={{0,64},{8,72},{16,80},{24,88},{32,96},{40,104},{48,112},{56,120},{... | collective-permute-start | bytes 442376 | tf_op jit(solution)/shard_map/ppermute | solution.py:17
  225.4 17.4 %copy-start.4 = (bf16[128,2048]{1,0:T(8,128)(2,1)}, bf16[128,2048]{1,0:T(8,128)(2,1)S(1)}, u32[]{:S(2)}) copy-start(bf16[128,2048]{1,0:T(8,128)(2,1)S(1)} %convolution_convert_fusion.2) | copy-start | bytes 1572868
  225.5 13.4 %collective-permute-start.5 = (bf16[128,576]{0,1:T(8,128)(2,1)S(1)}, bf16[128,576]{0,1:T(8,128)(2,1)S(1)}, u32[]{:S(2)}, u32[]{:S(2)}) collective-permute-start(bf16[128,576]{0,1:T(8,128)(2,1)S(1)} %collective-permute-done.4), channel_id=1, source_target_pairs={{0,64},{8,72},{16,80},{24,88},{32,96},{40,104},{48,112},{56,120},{... | collective-permute-start | bytes 442376 | tf_op jit(solution)/shard_map/ppermute | solution.py:17
  239.4 14.2 %copy-start.61 = (f32[32]{0:T(128)S(1)}, f32[32]{0:T(128)}, u32[]{:S(2)}) copy-start(f32[32]{0:T(128)} %multiply_power_fusion) | copy-start | bytes 388
  239.4 14.2 %copy-start.63 = (f32[128]{0:T(128)S(1)}, f32[128]{0:T(128)}, u32[]{:S(2)}) copy-start(f32[128]{0:T(128)} %get-tuple-element.8) | copy-start | bytes 1540
  239.4 14.2 %copy-start.64 = (f32[128]{0:T(128)S(1)}, f32[128]{0:T(128)}, u32[]{:S(2)}) copy-start(f32[128]{0:T(128)} %get-tuple-element.79) | copy-start | bytes 1540
  239.4 14.2 %copy-start.65 = (f32[128]{0:T(128)S(1)}, f32[128]{0:T(128)}, u32[]{:S(2)}) copy-start(f32[128]{0:T(128)} %get-tuple-element.80) | copy-start | bytes 1540
  239.5 14.2 %copy-start.76 = (f32[128]{0:T(128)S(1)}, f32[128]{0:T(128)}, u32[]{:S(2)}) copy-start(f32[128]{0:T(128)} %add_convert_fusion.9) | copy-start | bytes 1540
  239.6 12.5 %collective-permute-start.6 = (bf16[128,576]{0,1:T(8,128)(2,1)S(1)}, bf16[128,576]{0,1:T(8,128)(2,1)S(1)}, u32[]{:S(2)}, u32[]{:S(2)}) collective-permute-start(bf16[128,576]{0,1:T(8,128)(2,1)S(1)} %collective-permute-done.5), channel_id=1, source_target_pairs={{0,64},{8,72},{16,80},{24,88},{32,96},{40,104},{48,112},{56,120},{... | collective-permute-start | bytes 442376 | tf_op jit(solution)/shard_map/ppermute | solution.py:17
  271.9 53.0 %copy-start.31 = (bf16[128,32]{0,1:T(8,128)(2,1)S(1)}, bf16[128,32]{0,1:T(8,128)(2,1)}, u32[]{:S(2)}) copy-start(bf16[128,32]{0,1:T(8,128)(2,1)} %convolution_convert_fusion.8) | copy-start | bytes 24580
  339.1 7.5 copy-start.58
  339.1 7.6 copy-start.23
  339.1 7.8 copy-start.30
  339.1 46.2 %copy-start.20 = (bf16[128,1536]{1,0:T(8,128)(2,1)S(1)}, bf16[128,1536]{1,0:T(8,128)(2,1)}, u32[]{:S(2)}) copy-start(bf16[128,1536]{1,0:T(8,128)(2,1)} %param.12) | copy-start | bytes 1179652
  339.1 590.4 %copy-start.1 = (bf16[512,2048]{1,0:T(8,128)(2,1)S(1)}, bf16[512,2048]{1,0:T(8,128)(2,1)}, u32[]{:S(2)}) copy-start(bf16[512,2048]{1,0:T(8,128)(2,1)} %param.15) | copy-start | bytes 6291460
  (41 other events, 68.6 us)
Sparse Core Ops, SparseCore 0:
  15.9 122.0 all-gather.3
  386.3 536.9 all-reduce.3
